TPU v7x, 32 devices: a whole 2x2x4 slice. The times are simulated.
32 devices in a mesh: seq: 8 (over y, x, core), ch: 4 (over z).
Axes of the slice: x: 2, y: 2, z: 4, core: 2. Of those that a mesh axis runs over, the one named last changes fastest.
Arguments:
- inputs: bfloat16 [1536, 131072], P('ch', 'seq'), may hold values from -6 to 6
- gating: bfloat16 [1536, 131072], P('ch', 'seq'), may hold values from -6 to 6
- upstream: bfloat16 [1536, 131072], P('ch', 'seq'), may hold values from -6 to 6
- factor_one: bfloat16 [512, 512], replicated, may hold values from -0.25 to 0.25
- factor_two: bfloat16 [256, 256], replicated, may hold values from -0.375 to 0.375
- factor_three: bfloat16 [256, 256], replicated, may hold values from -0.375 to 0.375
- factor_four: bfloat16 [512, 512], replicated, may hold values from -0.25 to 0.25
- kernel_cols: float32 [1536, 512], P('ch'), may hold values from -4 to 4
- kernel_rows: float32 [1536, 256], P('ch'), may hold values from -4 to 4
Outputs:
- input_grad: bfloat16 [1536, 131072], P('ch', 'seq')
- gating_grad: bfloat16 [1536, 131072], P('ch', 'seq')
- one_grad: float32 [512, 512], replicated
- two_grad: float32 [256, 256], replicated
- three_grad: float32 [256, 256], replicated
- four_grad: float32 [512, 512], replicated
- cols_grad: float32 [1536, 512], P('ch')
- rows_grad: float32 [1536, 256], P('ch')
All inputs are finite; a program needn't handle non-finite values.
Results may differ from a plain program's by a relative error of at most 0.0076.
Values may be sent and summed in bfloat16 or wider, within the bound.
A program may use at most 384 MiB of HBM per device.

v0:
```python
import math

import jax
import jax.numpy as jnp
from jax import lax
from jax.sharding import PartitionSpec as P

P1 = 256
P2 = 512
C = 1536


def local(
    inputs,
    gating,
    upstream,
    factor_one,
    factor_two,
    factor_three,
    factor_four,
    kernel_cols,
    kernel_rows,
):
    width = inputs.shape[0]
    length = inputs.shape[1]
    parts = lax.axis_size("seq")
    flt = jnp.float32
    half = jnp.bfloat16
    rows_local = length // P2
    up_gate = (upstream.astype(flt) * gating.astype(flt)).astype(half)
    moved_in, moved_gate = (
        lax.all_to_all(inputs, "seq", split_axis=0, concat_axis=1, tiled=True),
        lax.all_to_all(up_gate, "seq", split_axis=0, concat_axis=1, tiled=True),
    )
    several = width // parts
    offset = lax.axis_index("seq") * several
    local_cols = lax.dynamic_slice_in_dim(kernel_cols, offset, several, 0)
    local_rows = lax.dynamic_slice_in_dim(kernel_rows, offset, several, 0)
    shaped = moved_in.reshape(several, P1, P2)
    gate_rows = moved_gate.reshape(several, P1, P2)
    first_prod = jnp.einsum("cij,jk->cik", shaped, factor_one, preferred_element_type=flt)
    first_out = (first_prod * local_cols[:, None, :]).astype(half)
    left_prod = jnp.einsum("ki,cij->ckj", factor_two, first_out, preferred_element_type=flt)
    left_out = (left_prod * local_rows[:, :, None]).astype(half)
    second = jnp.einsum("ki,cij->ckj", factor_three, left_out, preferred_element_type=flt).astype(
        half
    )
    grad_four = jnp.einsum("cij,cik->jk", second, gate_rows, preferred_element_type=flt)
    grad_second = jnp.einsum(
        "cik,jk->cij", gate_rows, factor_four, preferred_element_type=flt
    ).astype(half)
    grad_three = jnp.einsum("ckj,cij->ki", grad_second, left_out, preferred_element_type=flt)
    grad_left = jnp.einsum("ki,ckj->cij", factor_three, grad_second, preferred_element_type=flt)
    rows_part = jnp.sum(grad_left * left_prod, axis=2)
    grad_prod = (grad_left * local_rows[:, :, None]).astype(half)
    grad_two = jnp.einsum("ckj,cij->ki", grad_prod, first_out, preferred_element_type=flt)
    grad_first = jnp.einsum(
        "ki,ckj->cij", factor_two, grad_prod, preferred_element_type=flt
    ).astype(half)
    cols_part = jnp.sum(grad_first.astype(flt) * first_prod, axis=1)
    grad_inner = (grad_first.astype(flt) * local_cols[:, None, :]).astype(half)
    grad_one = jnp.einsum("cij,cik->jk", shaped, grad_inner, preferred_element_type=flt)
    local_input = jnp.einsum(
        "cik,jk->cij", grad_inner, factor_one, preferred_element_type=flt
    ).astype(half)
    input_grad, second_rows = (
        lax.all_to_all(
            local_input.reshape(several, P1 * P2), "seq", split_axis=1, concat_axis=0, tiled=True
        ),
        lax.all_to_all(
            second.reshape(several, P1 * P2), "seq", split_axis=1, concat_axis=0, tiled=True
        ),
    )
    cols_sum, rows_sum = (
        lax.all_gather(cols_part, "seq", axis=0, tiled=True),
        lax.all_gather(rows_part, "seq", axis=0, tiled=True),
    )
    final_prod = jnp.einsum(
        "cij,jk->cik",
        second_rows.reshape(width, rows_local, P2),
        factor_four,
        preferred_element_type=flt,
    )
    gating_grad = (
        (upstream.reshape(width, rows_local, P2).astype(flt) * final_prod)
        .astype(half)
        .reshape(width, length)
    )
    one_sum, two_sum, three_sum, four_sum = lax.psum(
        (grad_one, grad_two, grad_three, grad_four), ("seq", "ch")
    )
    scale_one = 1.0 / math.sqrt(P1 * C)
    scale_two = 1.0 / math.sqrt(P2 * C)
    return (
        input_grad,
        gating_grad,
        one_sum * scale_one,
        two_sum * scale_two,
        three_sum * scale_two,
        four_sum * scale_one,
        cols_sum / math.sqrt(P1),
        rows_sum / math.sqrt(P2),
    )


def solution(mesh):
    in_specs = (
        P("ch", "seq"),
        P("ch", "seq"),
        P("ch", "seq"),
        P(),
        P(),
        P(),
        P(),
        P("ch", None),
        P("ch", None),
    )
    out_specs = (P("ch", "seq"), P("ch", "seq"), P(), P(), P(), P(), P("ch", None), P("ch", None))
    return jax.shard_map(local, mesh=mesh, in_specs=in_specs, out_specs=out_specs, check_vma=False)
```

profile of v0, /device:TPU:0, one launch (start us, length us, event | category | flops | bytes accessed | tf_op | source)
XLA Modules:
  0.0 879.9 jit_solution(3477879930901490185)
XLA Ops:
  7.2 0.0 copy-start
  7.2 9.9 %multiply_convert_fusion.4 = bf16[384,16384]{1,0:T(8,128)(2,1)S(1)} fusion(bf16[384,16384]{1,0:T(8,128)(2,1)} %param.10, bf16[384,16384]{1,0:T(8,128)(2,1)} %param.11), kind=kLoop, calls=%fused_computation.9 | loop fusion | flops 25165824 | bytes 37748736 | tf_op jit(solution)/shard_map/convert_element_type | solution.py:30
  17.1 144.0 %all_to_all.67 = bf16[8,48,16384]{2,1,0:T(8,128)(2,1)} all-to-all(bf16[8,48,16384]{2,1,0:T(8,128)(2,1)S(1)} %bitcast.84), channel_id=1, replica_groups=mesh['seq'=8,'ch'=4] {'seq'}, dimensions={0} | all-to-all | bytes 25165824 | tf_op jit(solution)/shard_map/all_to_all | solution.py:33
  161.1 5.4 all-to-all-start.2
  166.5 0.8 constant_dynamic-slice_fusion.1
  167.3 14.4 %copy.71 = bf16[48,8,16384]{2,1,0:T(8,128)(2,1)} copy(bf16[48,8,16384]{2,0,1:T(8,128)(2,1)} %bitcast.82) | data formatting | bytes 25165824 | tf_op jit(solution)/shard_map/all_to_all | solution.py:33
  181.7 19.5 %reshape.52 = bf16[48,256,512]{2,1,0:T(8,128)(2,1)} reshape(bf16[48,8,16384]{2,1,0:T(8,128)(2,1)} %copy.71) | data formatting | bytes 25165824 | tf_op jit(solution)/shard_map/reshape | solution.py:40
  201.3 11.6 %convolution_convert_fusion.1 = bf16[48,256,512]{2,1,0:T(8,128)(2,1)S(1)} fusion(bf16[48,256,512]{2,1,0:T(8,128)(2,1)} %reshape.52, bf16[512,512]{1,0:T(8,128)(2,1)S(1)} %copy-done.4), kind=kOutput, calls=%fused_computation.19 | convolution fusion | flops 6448742400 | bytes 25690112 | tf_op jit(solution)/shard_map/cik,jk->cij/dot_general | solution.py:49
  212.8 4.5 copy-done.2
  217.4 10.1 %fusion.39 = f32[48,512,256]{2,1,0:T(8,128)} fusion(bf16[48,256,512]{2,1,0:T(8,128)(2,1)S(1)} %convolution_convert_fusion.1, bf16[256,256]{1,0:T(8,128)(2,1)S(1)} %copy-done.7), kind=kOutput, calls=%fused_computation.39 | convolution fusion | flops 3221225472 | bytes 37879808 | tf_op jit(solution)/shard_map/ki,ckj->cij/dot_general | solution.py:53
  227.5 14.8 %convolution_convert_fusion = bf16[48,512,256]{1,2,0:T(8,128)(2,1)} fusion(f32[48,512,256]{2,1,0:T(8,128)} %fusion.39, f32[48,256]{1,0:T(8,128)S(1)} %constant_dynamic-slice_fusion.1, bf16[256,256]{1,0:T(8,128)(2,1)S(1)} %copy-done.6), kind=kOutput, calls=%fused_computation.17 | convolution fusion | flops 3240099840 | bytes 37928960 | tf_op jit(solution)/shard_map/ki,ckj->cij/dot_general | solution.py:57
  242.3 14.4 %fusion.10 = bf16[48,256,512]{2,1,0:T(8,128)(2,1)} fusion(bf16[48,512,256]{1,2,0:T(8,128)(2,1)} %convolution_convert_fusion, f32[48,512]{1,0:T(8,128)S(1)} %constant_dynamic-slice_fusion, bf16[512,512]{1,0:T(8,128)(2,1)S(1)} %copy-done.3), kind=kOutput, calls=%fused_computation.18 | convolution fusion | flops 6467616768 | bytes 25788416 | tf_op jit(solution)/shard_map/cik,jk->cij/dot_general | solution.py:63
  256.7 19.8 %all_to_all.53 = bf16[48,8,16384]{2,1,0:T(8,128)(2,1)} reshape(bf16[48,256,512]{2,1,0:T(8,128)(2,1)} %fusion.10) | data formatting | bytes 25165824 | tf_op jit(solution)/shard_map/all_to_all | solution.py:67
  276.5 14.5 %copy.75 = bf16[48,8,16384]{2,0,1:T(8,128)(2,1)} copy(bf16[48,8,16384]{2,1,0:T(8,128)(2,1)} %all_to_all.53) | data formatting | bytes 25165824 | tf_op jit(solution)/shard_map/all_to_all | solution.py:67
  291.0 14.5 %all-to-all-done.2 = bf16[8,48,16384]{2,1,0:T(8,128)(2,1)} async-done(((bf16[8,48,16384]{2,1,0:T(8,128)(2,1)}), bf16[8,48,16384]{2,1,0:T(8,128)(2,1)}, u32[]{:S(2)}, u32[]{:S(2)}) %all-to-all-start.2) | async-done | bytes 12582944 | tf_op jit(solution)/shard_map/all_to_all | solution.py:32
  305.4 5.3 all-to-all-start.1
  310.8 17.6 %copy.76 = f32[384,16384]{0,1:T(8,128)} copy(bf16[384,16384]{1,0:T(8,128)(2,1)} %param.11) | data formatting | bytes 37748736 | tf_op jit(solution)/shard_map/convert_element_type | solution.py:30
  328.4 24.6 %copy.82 = f32[384,32,512]{2,0,1:T(8,128)} copy(f32[384,32,512]{0,2,1:T(8,128)} %bitcast.80) | data formatting | bytes 50331648 | tf_op jit(solution)/shard_map/convert_element_type | solution.py:85
  353.0 14.4 %copy.77 = bf16[48,8,16384]{2,1,0:T(8,128)(2,1)} copy(bf16[48,8,16384]{2,0,1:T(8,128)(2,1)} %bitcast.12) | data formatting | bytes 25165824 | tf_op jit(solution)/shard_map/all_to_all | solution.py:32
  367.4 19.5 %reshape.53 = bf16[48,256,512]{2,1,0:T(8,128)(2,1)} reshape(bf16[48,8,16384]{2,1,0:T(8,128)(2,1)} %copy.77) | data formatting | bytes 25165824 | tf_op jit(solution)/shard_map/reshape | solution.py:39
  387.0 18.9 %fusion.1 = (f32[48,512]{1,0:T(8,128)}, f32[48,256,512]{2,1,0:T(8,128)}) fusion(bf16[48,512,256]{1,2,0:T(8,128)(2,1)} %convolution_convert_fusion, bf16[48,256,512]{2,1,0:T(8,128)(2,1)} %reshape.53, bf16[512,512]{1,0:T(8,128)(2,1)S(1)} %copy-done.3), kind=kOutput, calls=%fused_computation.3 | convolution fusion | flops 6461300736 | bytes 50954240 | tf_op jit(solution)/shard_map/cij,jk->cik/dot_general | solution.py:41
  405.9 16.3 %fusion.21 = f32[48,512,256]{2,1,0:T(8,128)} fusion(f32[48,256,512]{2,1,0:T(8,128)} %get-tuple-element.45, f32[48,512]{1,0:T(8,128)S(1)} %constant_dynamic-slice_fusion, bf16[256,256]{1,0:T(8,128)(2,1)S(1)} %copy-done.6), kind=kOutput, calls=%fused_computation.22 | convolution fusion | flops 3233808384 | bytes 50561024 | tf_op jit(solution)/shard_map/ki,cij->ckj/dot_general | solution.py:43
  422.2 14.5 %convert_bitcast_fusion = bf16[48,256,512]{1,2,0:T(8,128)(2,1)} fusion(f32[48,512,256]{2,1,0:T(8,128)} %fusion.21, f32[48,256]{1,0:T(8,128)S(1)} %constant_dynamic-slice_fusion.1, bf16[256,256]{1,0:T(8,128)(2,1)S(1)} %copy-done.7), kind=kOutput, calls=%fused_computation.14 | convolution fusion | flops 3240099840 | bytes 37928960 | tf_op jit(solution)/shard_map/ki,cij->ckj/dot_general | solution.py:45
  436.7 16.7 %copy.79 = bf16[48,256,512]{2,1,0:T(8,128)(2,1)} copy(bf16[48,256,512]{1,2,0:T(8,128)(2,1)} %convert_bitcast_fusion) | data formatting | bytes 25165824 | tf_op jit(solution)/shard_map/convert_element_type | solution.py:45
  453.4 19.5 %all_to_all.60 = bf16[48,8,16384]{2,1,0:T(8,128)(2,1)} reshape(bf16[48,256,512]{2,1,0:T(8,128)(2,1)} %copy.79) | data formatting | bytes 25165824 | tf_op jit(solution)/shard_map/all_to_all | solution.py:70
  472.9 26.0 %copy.80 = bf16[48,8,16384]{2,0,1:T(8,128)(2,1)} copy(bf16[48,8,16384]{2,1,0:T(8,128)(2,1)} %all_to_all.60) | data formatting | bytes 25165824 | tf_op jit(solution)/shard_map/all_to_all | solution.py:70
  499.0 16.0 %fusion.28 = f32[256,256]{1,0:T(8,128)} fusion(bf16[48,256,512]{2,1,0:T(8,128)(2,1)} %copy-done.2, f32[48,512,256]{2,1,0:T(8,128)} %fusion.21, f32[48,256]{1,0:T(8,128)S(1)} %constant_dynamic-slice_fusion.1), kind=kOutput, calls=%fused_computation.26 | convolution fusion | flops 3233808384 | bytes 38060032 | tf_op jit(solution)/shard_map/ckj,cij->ki/dot_general | solution.py:52
  514.9 5.3 all-to-all-start.3
  520.3 0.0 all-reduce.3.cloned.1.call-start
  520.3 14.1 %fusion.22 = f32[512,512]{0,1:T(8,128)} fusion(bf16[48,256,512]{2,1,0:T(8,128)(2,1)} %reshape.53, bf16[48,512,256]{1,2,0:T(8,128)(2,1)} %convolution_convert_fusion, f32[48,512]{1,0:T(8,128)S(1)} %constant_dynamic-slice_fusion), kind=kOutput, calls=%fused_computation.23 | convolution fusion | flops 6461325312 | bytes 26312704 | tf_op jit(solution)/shard_map/cij,cik->jk/dot_general | solution.py:62
  534.4 12.6 %convolution_bitcast_fusion = f32[512,512]{0,1:T(8,128)} fusion(bf16[48,256,512]{1,2,0:T(8,128)(2,1)} %convert_bitcast_fusion, bf16[48,256,512]{2,1,0:T(8,128)(2,1)} %reshape.52), kind=kOutput, calls=%fused_computation.24 | convolution fusion | flops 6442450944 | bytes 26214400 | tf_op jit(solution)/shard_map/cij,cik->jk/dot_general | solution.py:48
  547.0 17.6 %fusion.25 = f32[256,256]{1,0:T(8,128)} fusion(f32[48,256,512]{2,1,0:T(8,128)} %get-tuple-element.45, f32[48,512]{1,0:T(8,128)S(1)} %constant_dynamic-slice_fusion, f32[48,512,256]{2,1,0:T(8,128)} %fusion.39, f32[48,256]{1,0:T(8,128)S(1)} %constant_dynamic-slice_fusion.1), kind=kOutput, calls=%fused_computation.25 | convolution fusion | flops 3246391296 | bytes 50741248 | tf_op jit(solution)/shard_map/ckj,cij->ki/dot_general | solution.py:56
  564.6 0.0 all-reduce.3.cloned.1.call-update
  564.6 16.7 %multiply_reduce_fusion = f32[48,256]{1,0:T(8,128)S(1)} fusion(f32[48,512,256]{2,1,0:T(8,128)} %fusion.39, f32[48,512,256]{2,1,0:T(8,128)} %fusion.21), kind=kLoop, calls=%fused_computation.4 | loop fusion | flops 12570624 | bytes 50380800 | tf_op jit(solution)/shard_map/reduce_sum | solution.py:54
  581.3 89.7 %all_gather.7 = f32[384,256]{1,0:T(8,128)S(1)} all-gather(f32[48,256]{1,0:T(8,128)S(1)} %multiply_reduce_fusion), channel_id=1, replica_groups=mesh['seq'=8,'ch'=4] {'seq'}, dimensions={0}, use_global_device_ids=true | all-gather | bytes 442368 | tf_op jit(solution)/shard_map/all_gather | solution.py:76
  671.0 9.2 %all_gather.6 = f32[384,512]{1,0:T(8,128)S(1)} all-gather(f32[48,512]{1,0:T(8,128)S(1)} %copy-done.8), channel_id=1, replica_groups=mesh['seq'=8,'ch'=4] {'seq'}, dimensions={0}, use_global_device_ids=true | all-gather | bytes 884736 | tf_op jit(solution)/shard_map/all_gather | solution.py:75
  680.2 0.8 broadcast_multiply_fusion.3
  681.0 0.9 broadcast_multiply_fusion.2
  682.0 62.6 %all-reduce.3.cloned.1.call-done = (f32[512,512]{0,1:T(8,128)}, f32[256,256]{1,0:T(8,128)}, f32[256,256]{1,0:T(8,128)}, f32[512,512]{0,1:T(8,128)}) async-done(((f32[512,512]{0,1:T(8,128)}, f32[256,256]{1,0:T(8,128)}, f32[256,256]{1,0:T(8,128)}, f32[512,512]{0,1:T(8,128)}), (f32[512,512]{0,1:T(8,128)}, f32[256,256]{1,0:T(8,128)}, f32[256,256]{1,0:T(8,128)}, ...) | async-done | bytes 2621456 | tf_op jit(solution)/shard_map/psum | solution.py:89
  744.5 1.8 broadcast_multiply_fusion
  746.3 1.3 copy.90
  747.6 1.3 copy.89
  748.9 1.9 broadcast_multiply_fusion.4
  750.8 12.8 %copy.101 = bf16[48,8,32,512]{3,2,1,0:T(8,128)(2,1)} copy(bf16[48,8,32,512]{3,1,2,0:T(8,128)(2,1)} %bitcast.26) | data formatting | bytes 25165824
  763.6 65.3 %multiply_convert_fusion = bf16[384,32,512]{2,0,1:T(8,128)(2,1)} fusion(f32[384,32,512]{2,0,1:T(8,128)} %copy.82, bf16[384,32,512]{2,1,0:T(8,128)(2,1)} %bitcast.81, bf16[512,512]{1,0:T(8,128)(2,1)S(1)} %copy-done.5), kind=kOutput, calls=%fused_computation.5 | convolution fusion | flops 6455033856 | bytes 50855936 | tf_op jit(solution)/shard_map/cij,jk->cik/dot_general | solution.py:78
  828.9 16.7 %copy.83 = bf16[384,32,512]{0,2,1:T(8,128)(2,1)} copy(bf16[384,32,512]{2,0,1:T(8,128)(2,1)} %multiply_convert_fusion) | data formatting | bytes 25165824 | tf_op jit(solution)/shard_map/convert_element_type | solution.py:86
  845.6 16.6 %copy.88 = bf16[384,16384]{1,0:T(8,128)(2,1)} copy(bf16[384,16384]{0,1:T(8,128)(2,1)} %bitcast.83) | data formatting | bytes 25165824
  862.2 10.5 %copy.111 = bf16[384,16384]{1,0:T(8,128)(2,1)} copy(bf16[384,16384]{1,0:T(8,128)(2,1)} %bitcast.9) | data formatting | bytes 25165824
  (19 shorter events, 0.0 us)
Async XLA Ops:
  7.2 160.1 %copy-start = (f32[384,512]{1,0:T(8,128)S(1)}, f32[384,512]{1,0:T(8,128)}, u32[]{:S(2)}) copy-start(f32[384,512]{1,0:T(8,128)} %param.16) | copy-start | bytes 2359300
  161.1 144.4 %all-to-all-start.2 = ((bf16[8,48,16384]{2,1,0:T(8,128)(2,1)}), bf16[8,48,16384]{2,1,0:T(8,128)(2,1)}, u32[]{:S(2)}, u32[]{:S(2)}) async-start(bf16[8,48,16384]{2,1,0:T(8,128)(2,1)} %bitcast.85), calls=%async_computation.2 | async-start | bytes 25165824 | tf_op jit(solution)/shard_map/all_to_all | solution.py:32
  181.7 19.5 %copy-start.4 = (bf16[512,512]{1,0:T(8,128)(2,1)S(1)}, bf16[512,512]{1,0:T(8,128)(2,1)}, u32[]{:S(2)}) copy-start(bf16[512,512]{1,0:T(8,128)(2,1)} %param.15) | copy-start | bytes 1572868
  201.3 16.1 %copy-start.7 = (bf16[256,256]{1,0:T(8,128)(2,1)S(1)}, bf16[256,256]{1,0:T(8,128)(2,1)}, u32[]{:S(2)}) copy-start(bf16[256,256]{1,0:T(8,128)(2,1)} %param.14) | copy-start | bytes 393220
  212.8 4.5 copy-start.2
  217.4 10.1 %copy-start.6 = (bf16[256,256]{1,0:T(8,128)(2,1)S(1)}, bf16[256,256]{1,0:T(8,128)(2,1)}, u32[]{:S(2)}) copy-start(bf16[256,256]{1,0:T(8,128)(2,1)} %param.13) | copy-start | bytes 393220
  227.5 14.8 %copy-start.3 = (bf16[512,512]{1,0:T(8,128)(2,1)S(1)}, bf16[512,512]{1,0:T(8,128)(2,1)}, u32[]{:S(2)}) copy-start(bf16[512,512]{1,0:T(8,128)(2,1)} %param.12) | copy-start | bytes 1572868
  305.4 209.5 %all-to-all-start.1 = ((bf16[48,8,16384]{2,0,1:T(8,128)(2,1)}), bf16[48,8,16384]{2,0,1:T(8,128)(2,1)}, u32[]{:S(2)}, u32[]{:S(2)}) async-start(bf16[48,8,16384]{2,0,1:T(8,128)(2,1)} %copy.75), calls=%async_computation.1 | async-start | bytes 25165824 | tf_op jit(solution)/shard_map/all_to_all | solution.py:67
  514.9 235.9 %all-to-all-start.3 = ((bf16[48,8,16384]{2,0,1:T(8,128)(2,1)}), bf16[48,8,16384]{2,0,1:T(8,128)(2,1)}, u32[]{:S(2)}, u32[]{:S(2)}) async-start(bf16[48,8,16384]{2,0,1:T(8,128)(2,1)} %copy.80), calls=%async_computation.3 | async-start | bytes 25165824 | tf_op jit(solution)/shard_map/all_to_all | solution.py:70
  520.3 224.3 %all-reduce.3.cloned.1.call-start = ((), (), s32[]{:S(2)}) async-start(), calls=%async_computation.4 | async-start | bytes 5242880 | tf_op jit(solution)/shard_map/psum | solution.py:89
  564.6 106.4 %copy-start.8 = (f32[48,512]{1,0:T(8,128)S(1)}, f32[48,512]{1,0:T(8,128)}, u32[]{:S(2)}) copy-start(f32[48,512]{1,0:T(8,128)} %get-tuple-element.44) | copy-start | bytes 294916
  750.8 12.8 %copy-start.5 = (bf16[512,512]{1,0:T(8,128)(2,1)S(1)}, bf16[512,512]{1,0:T(8,128)(2,1)}, u32[]{:S(2)}) copy-start(bf16[512,512]{1,0:T(8,128)(2,1)} %param.15) | copy-start | bytes 1572868
  862.2 10.5 %copy-start.1 = (f32[384,512]{1,0:T(8,128)S(1)}, f32[384,512]{1,0:T(8,128)}, u32[]{:S(2)}) copy-start(f32[384,512]{1,0:T(8,128)} %param.16) | copy-start | bytes 2359300
Sparse Core Ops, SparseCore 0:
  564.7 179.7 all-reduce.2
where the time goes:
time: 894 us; the launch traced here: 880 us
  local copies, waits for them, and re-layouts  271 us (30%)
  blocking collectives  243 us (27%)
  matrix products  226 us (25%)
  waiting for transfers between devices  77.1 us (9%)
  other arithmetic  31.9 us (4%)
  starting transfers between devices  16.1 us (2%)
  between operations  14.5 us (2%)
    all_to_all x1, blocking collectives, local(): lax.all_to_all(up_gate, 'seq', split_axis=0, concat_axis=1, tiled=True)  144 us
    all_gather x1, blocking collectives, local(): lax.all_gather(rows_part, 'seq', axis=0, tiled=True)  89.7 us
    dot_general x1, matrix products, local(): jnp.einsum('cij,jk->cik', second_rows.reshape(width, rows_local, P2), fac...  65.3 us
    psum x1, waiting for transfers between devices, local(): lax.psum((grad_one, grad_two, grad_three, grad_four), ('seq', 'ch'))  62.6 us
    unnamed x23, local copies, waits for them, and re-layouts  47.1 us
    all_to_all x2, local copies, waits for them, and re-layouts, local(): lax.all_to_all(second.reshape(several, P1 * P2), 'seq', split_axis=1, con...  45.5 us
    all_to_all x2, local copies, waits for them, and re-layouts, local(): lax.all_to_all(local_input.reshape(several, P1 * P2), 'seq', split_axis=1...  34.3 us
    convert_element_type x1, local copies, waits for them, and re-layouts, local(): upstream.reshape(width, rows_local, P2).astype(flt) * final_prod  24.6 us
  transfers between devices with their start and end apart: 4, of which 2 were waited for; matrix products, arithmetic and copies ran while one was open for 40% of the time, Pallas kernels for 0%

commit v1 on v0

v1 whole, which is shorter than its diff:
```python
import math

import jax
import jax.numpy as jnp
from jax import lax
from jax.experimental import pallas as pl
from jax.experimental.pallas import tpu as pltpu
from jax.sharding import PartitionSpec as P

P1 = 256
P2 = 512
C = 1536
LANES = 128
TALL = 16
FLT = jnp.float32
HALF = jnp.bfloat16


def nn(a, b):
    return lax.dot_general(a, b, (((1,), (0,)), ((), ())), preferred_element_type=FLT)


def nt(a, b):
    return lax.dot_general(a, b, (((1,), (1,)), ((), ())), preferred_element_type=FLT)


def tn(a, b):
    return lax.dot_general(a, b, (((0,), (0,)), ((), ())), preferred_element_type=FLT)


def gather_rows(ref, rows):
    return jnp.concatenate([ref[:, i * P2 : (i + 1) * P2] for i in range(rows)], axis=0)


def to_channels(value, swap, out_ref, rows):
    for v in range(P2 // LANES):
        swap[v] = value[:, v * LANES : (v + 1) * LANES]
    for c in range(TALL):
        for v in range(P2 // LANES):
            out_ref[c, :, v * LANES : (v + 1) * LANES] = swap[
                v, pl.ds(c, rows, stride=TALL), :
            ].astype(HALF)


def to_rows(in_ref, swap, rows):
    for c in range(TALL):
        for v in range(P2 // LANES):
            swap[v, c * rows : (c + 1) * rows, :] = in_ref[
                c, :, v * LANES : (v + 1) * LANES
            ].astype(FLT)
    return jnp.concatenate(
        [
            jnp.concatenate(
                [swap[v, pl.ds(i, TALL, stride=rows), :].astype(HALF) for i in range(rows)], axis=0
            )
            for v in range(P2 // LANES)
        ],
        axis=1,
    )


def gated(up_ref, gate_ref, rows):
    return jnp.concatenate(
        [
            (
                up_ref[:, i * P2 : (i + 1) * P2].astype(FLT)
                * gate_ref[:, i * P2 : (i + 1) * P2].astype(FLT)
            ).astype(HALF)
            for i in range(rows)
        ],
        axis=0,
    )


def grad_second_body(up_ref, gate_ref, four_ref, out_ref, swap):
    rows = out_ref.shape[1]
    to_channels(nt(gated(up_ref, gate_ref, rows), four_ref[...]), swap, out_ref, rows)


def first_body(in_ref, one_ref, cols_ref, out_ref, swap):
    rows = out_ref.shape[1]
    prod = nn(gather_rows(in_ref, rows), one_ref[...])
    scaled = prod.reshape(rows, TALL, P2) * cols_ref[...][None]
    to_channels(scaled.reshape(rows * TALL, P2), swap, out_ref, rows)


def second_body(first_ref, two_ref, three_ref, rows_ref, out_ref):
    parts, several, rows, _ = first_ref.shape
    for c in range(several):
        first = first_ref[:, c].reshape(parts * rows, P2)
        left = (nn(two_ref[...], first) * rows_ref[c]).astype(HALF)
        out_ref[:, c] = nn(three_ref[...], left).astype(HALF).reshape(parts, rows, P2)


def middle_body(
    first_ref,
    grad_ref,
    two_ref,
    two_t_ref,
    three_t_ref,
    rows_ref,
    out_ref,
    rows_out,
    two_out,
    three_out,
):
    parts, several, rows, _ = first_ref.shape

    @pl.when(pl.program_id(0) == 0)
    def _():
        two_out[...] = jnp.zeros_like(two_out)
        three_out[...] = jnp.zeros_like(three_out)

    for c in range(several):
        first = first_ref[:, c].reshape(parts * rows, P2)
        grad_second = grad_ref[:, c].reshape(parts * rows, P2)
        scale = rows_ref[c]
        left_prod = nn(two_ref[...], first)
        left = (left_prod * scale).astype(HALF)
        grad_left = nn(three_t_ref[...], grad_second)
        three_out[...] += nt(grad_second, left)
        rows_out[c] = jnp.sum(grad_left * left_prod, axis=1, keepdims=True)
        grad_prod = (grad_left * scale).astype(HALF)
        two_out[...] += nt(grad_prod, first)
        out_ref[:, c] = nn(two_t_ref[...], grad_prod).astype(HALF).reshape(parts, rows, P2)


def gating_body(second_ref, up_ref, gate_ref, four_ref, out_ref, four_out, swap):
    rows = second_ref.shape[1]

    @pl.when(pl.program_id(0) == 0)
    def _():
        four_out[...] = jnp.zeros_like(four_out)

    second = to_rows(second_ref, swap, rows)
    final = nn(second, four_ref[...])
    for i in range(rows):
        up = up_ref[:, i * P2 : (i + 1) * P2].astype(FLT)
        out_ref[:, i * P2 : (i + 1) * P2] = (up * final[i * TALL : (i + 1) * TALL]).astype(HALF)
    four_out[...] += tn(second, gated(up_ref, gate_ref, rows))


def input_body(grad_ref, in_ref, one_ref, one_t_ref, cols_ref, out_ref, cols_out, one_out, swap):
    rows = grad_ref.shape[1]

    @pl.when(pl.program_id(0) == 0)
    def _():
        one_out[...] = jnp.zeros_like(one_out)

    grad_first = to_rows(grad_ref, swap, rows).astype(FLT).reshape(rows, TALL, P2)
    shaped = gather_rows(in_ref, rows)
    prod = nn(shaped, one_ref[...]).reshape(rows, TALL, P2)
    cols_out[...] = jnp.sum(grad_first * prod, axis=0)
    inner = (grad_first * cols_ref[...][None]).astype(HALF).reshape(rows * TALL, P2)
    one_out[...] += tn(shaped, inner)
    back = nn(inner, one_t_ref[...]).astype(HALF)
    for i in range(rows):
        out_ref[:, i * P2 : (i + 1) * P2] = back[i * TALL : (i + 1) * TALL]


def call(body, name, grid, in_specs, out_specs, out_shape, scratch, flops, moved, args):
    return pl.pallas_call(
        body,
        name=name,
        grid=(grid,),
        in_specs=in_specs,
        out_specs=out_specs,
        out_shape=out_shape,
        scratch_shapes=scratch,
        compiler_params=pltpu.CompilerParams(
            dimension_semantics=("arbitrary",), vmem_limit_bytes=48 * 2**20
        ),
        cost_estimate=pl.CostEstimate(flops=flops, bytes_accessed=moved, transcendentals=0),
    )(*args)


def local(
    inputs,
    gating,
    upstream,
    factor_one,
    factor_two,
    factor_three,
    factor_four,
    kernel_cols,
    kernel_rows,
):
    width, length = inputs.shape
    parts = lax.axis_size("seq")
    rows = length // P2
    several = width // parts
    few = math.gcd(several, 4)
    tall_grid = width // TALL
    wide_grid = several // few
    size = width * length

    flat = pl.BlockSpec((TALL, length), lambda g: (g, 0))
    cube = pl.BlockSpec((TALL, rows, P2), lambda g: (g, 0, 0))
    cols_spec = pl.BlockSpec((TALL, P2), lambda g: (g, 0))
    big = pl.BlockSpec((P2, P2), lambda g: (0, 0))
    small = pl.BlockSpec((P1, P1), lambda g: (0, 0))
    group = pl.BlockSpec((parts, few, rows, P2), lambda g: (0, g, 0, 0))
    rows_spec = pl.BlockSpec((few, P1, 1), lambda g: (g, 0, 0))
    swap = [pltpu.VMEM((P2 // LANES, rows * TALL, LANES), FLT)]
    cube_shape = jax.ShapeDtypeStruct((width, rows, P2), HALF)
    group_shape = jax.ShapeDtypeStruct((parts, several, rows, P2), HALF)
    flat_shape = jax.ShapeDtypeStruct((width, length), HALF)
    big_shape = jax.ShapeDtypeStruct((P2, P2), FLT)
    small_shape = jax.ShapeDtypeStruct((P1, P1), FLT)
    wide = 2 * size * P2
    tall = 2 * size * P1

    def exchange(x):
        return lax.all_to_all(
            x.reshape(parts, several, rows, P2), "seq", split_axis=0, concat_axis=0
        )

    offset = lax.axis_index("seq") * several
    local_rows = lax.dynamic_slice_in_dim(kernel_rows, offset, several, 0)[:, :, None]

    grad_second = call(
        grad_second_body, "grad_second", tall_grid, [flat, flat, big], cube, cube_shape, swap,
        wide, 6 * size, (upstream, gating, factor_four),
    )
    grad_moved = exchange(grad_second)
    first = call(
        first_body, "first", tall_grid, [flat, big, cols_spec], cube, cube_shape, swap,
        wide, 4 * size, (inputs, factor_one, kernel_cols),
    )
    first_moved = exchange(first)
    second = call(
        second_body, "second", wide_grid, [group, small, small, rows_spec], group, group_shape, [],
        2 * tall, 4 * size, (first_moved, factor_two, factor_three, local_rows),
    )
    second_moved = exchange(second).reshape(width, rows, P2)
    grad_first, rows_part, grad_two, grad_three = call(
        middle_body, "middle", wide_grid, [group, group, small, small, small, rows_spec],
        [group, rows_spec, small, small],
        [group_shape, jax.ShapeDtypeStruct((several, P1, 1), FLT), small_shape, small_shape], [],
        5 * tall, 6 * size,
        (first_moved, grad_moved, factor_two, factor_two.T, factor_three.T, local_rows),
    )
    grad_first_moved = exchange(grad_first).reshape(width, rows, P2)
    gating_grad, grad_four = call(
        gating_body, "gating", tall_grid, [cube, flat, flat, big], [flat, big],
        [flat_shape, big_shape], swap,
        2 * wide, 8 * size, (second_moved, upstream, gating, factor_four),
    )
    input_grad, cols_part, grad_one = call(
        input_body, "input", tall_grid, [cube, flat, big, big, cols_spec],
        [flat, cols_spec, big],
        [flat_shape, jax.ShapeDtypeStruct((width, P2), FLT), big_shape], swap,
        3 * wide, 6 * size,
        (grad_first_moved, inputs, factor_one, factor_one.T, kernel_cols),
    )
    rows_whole = lax.dynamic_update_slice_in_dim(
        jnp.zeros((width, P1), FLT), rows_part[:, :, 0], offset, 0
    )
    rows_sum = lax.psum(rows_whole, "seq")
    two_sum, three_sum, four_sum = lax.psum((grad_two, grad_three, grad_four), ("seq", "ch"))
    cols_sum = lax.psum(cols_part, "seq")
    one_sum = lax.psum(grad_one, ("seq", "ch"))
    scale_one = 1.0 / math.sqrt(P1 * C)
    scale_two = 1.0 / math.sqrt(P2 * C)
    return (
        input_grad,
        gating_grad,
        one_sum * scale_one,
        two_sum * scale_two,
        three_sum * scale_two,
        four_sum * scale_one,
        cols_sum / math.sqrt(P1),
        rows_sum / math.sqrt(P2),
    )


def solution(mesh):
    in_specs = (
        P("ch", "seq"),
        P("ch", "seq"),
        P("ch", "seq"),
        P(),
        P(),
        P(),
        P(),
        P("ch", None),
        P("ch", None),
    )
    out_specs = (P("ch", "seq"), P("ch", "seq"), P(), P(), P(), P(), P("ch", None), P("ch", None))
    return jax.shard_map(local, mesh=mesh, in_specs=in_specs, out_specs=out_specs, check_vma=False)
```

time: 894 us -> 840 us (0.940); the launches traced: 880 us -> 837 us
  waiting for transfers between devices: 77.1 us -> 597 us
  local copies, waits for them, and re-layouts: 271 us -> 6.71 us
  blocking collectives: 243 us -> 0 us
  matrix products: 226 us -> 0 us
  Pallas kernels: 0 us -> 184 us
  other arithmetic: 31.9 us -> 13.3 us
    all_to_all x3 -> x4, waiting for transfers between devices: 14.5 us -> 464 us  [exchange(): lax.all_to_all(x.reshape(parts, several, rows, P2), 'seq', split_axis=0,...]
    dot_general x12 -> x0, matrix products: 226 us -> none  [the longest x1 65.3 us: local(): jnp.einsum('cij,jk->cik', second_rows.reshape(width, rows_local, P2), fac...]
    pallas_call x0 -> x6, Pallas kernels: none -> 184 us  [call(): pl.pallas_call(body, name=name, grid=(grid,), in_specs=in_specs, out_spec...]
    all_to_all x1 -> x0, blocking collectives: 144 us -> none  [local(): lax.all_to_all(up_gate, 'seq', split_axis=0, concat_axis=1, tiled=True)]
    all_to_all x6 -> x0, local copies, waits for them, and re-layouts: 109 us -> none  [the longest x2 45.5 us: local(): lax.all_to_all(second.reshape(several, P1 * P2), 'seq', split_axis=1, con...]
    all_gather x2 -> x0, blocking collectives: 98.9 us -> none  [the longest x1 89.7 us: local(): lax.all_gather(rows_part, 'seq', axis=0, tiled=True)]
    convert_element_type x4 -> x0, local copies, waits for them, and re-layouts: 75.6 us -> none  [the longest x1 24.6 us: local(): upstream.reshape(width, rows_local, P2).astype(flt) * final_prod]
    psum x1 -> x2, waiting for transfers between devices: 62.6 us -> 133 us  [the longest x1 133 us: local(): one_sum = lax.psum(grad_one, ('seq', 'ch'))]
  transfers between devices with their start and end apart: 4 -> 6, of which waited for: 2 -> 5; matrix products, arithmetic and copies ran while one was open for 40% -> 2% of each run, Pallas kernels for 0% -> 16%
where the time goes in v1:
time: 840 us; the launch traced here: 837 us
  waiting for transfers between devices  597 us (71%)
  Pallas kernels  184 us (22%)
  starting transfers between devices  21.8 us (3%)
  between operations  14.2 us (2%)
  other arithmetic  13.3 us (2%)
    all_to_all x4, waiting for transfers between devices, exchange(): lax.all_to_all(x.reshape(parts, several, rows, P2), 'seq', split_axis=0,...  464 us
    pallas_call x6, Pallas kernels, call(): pl.pallas_call(body, name=name, grid=(grid,), in_specs=in_specs, out_spec...  184 us
    psum x1, waiting for transfers between devices, local(): one_sum = lax.psum(grad_one, ('seq', 'ch'))  133 us
    all_to_all x4, starting transfers between devices, exchange(): lax.all_to_all(x.reshape(parts, several, rows, P2), 'seq', split_axis=0,...  21.7 us
  transfers between devices with their start and end apart: 6, of which 5 were waited for; matrix products, arithmetic and copies ran while one was open for 2% of the time, Pallas kernels for 16%

profile of v1, /device:TPU:0, one launch (start us, length us, event | category | flops | bytes accessed | tf_op | source)
XLA Modules:
  0.0 836.8 jit_solution(462127345143260779)
XLA Ops:
  7.2 0.0 copy-start
  7.2 0.0 copy-start.2
  7.2 1.1 copy-done.2
  8.3 0.0 copy-start.4
  8.3 1.1 copy-done.4
  9.4 25.9 %first.1 = bf16[384,32,512]{2,1,0:T(8,128)(2,1)} custom-call(bf16[384,16384]{1,0:T(8,128)(2,1)} %in_ref.3, bf16[512,512]{1,0:T(8,128)(2,1)S(1)} %copy-done.2, f32[384,512]{1,0:T(8,128)S(1)} %copy-done.4), custom_call_target="tpu_custom_call" | custom-call | flops 6442450944 | bytes 25165824 | tf_op jit(solution)/shard_map/first/pallas_call | solution.py:162
  35.3 0.0 copy-start.6
  35.3 5.5 all-to-all-start
  40.8 0.0 copy-done.6
  40.8 28.4 %grad_second.1 = bf16[384,32,512]{2,1,0:T(8,128)(2,1)} custom-call(bf16[384,16384]{1,0:T(8,128)(2,1)} %up_ref.3, bf16[384,16384]{1,0:T(8,128)(2,1)} %gate_ref.3, bf16[512,512]{1,0:T(8,128)(2,1)S(1)} %copy-done.6), custom_call_target="tpu_custom_call" | custom-call | flops 6442450944 | bytes 37748736 | tf_op jit(solution)/shard_map/grad_second/pallas_call | solution.py:162
  69.3 111.3 %all-to-all-done.first_ref = bf16[8,48,32,512]{3,2,1,0:T(8,128)(2,1)} async-done(((bf16[8,48,32,512]{3,2,1,0:T(8,128)(2,1)}), bf16[8,48,32,512]{3,2,1,0:T(8,128)(2,1)}, u32[]{:S(2)}, u32[]{:S(2)}) %all-to-all-start) | async-done | bytes 12582944 | tf_op jit(solution)/shard_map/all_to_all | solution.py:214
  180.6 0.0 copy-start.7
  180.6 0.0 copy-start.8
  180.6 5.5 all-to-all-start.1
  186.1 0.0 copy-done
  186.1 4.0 copy.22.rows_ref
  190.1 0.0 copy-done.7
  190.1 0.1 copy.20
  190.2 0.0 copy-done.8
  190.2 0.1 copy.21
  190.3 134.7 %all-to-all-done.1.grad_ref = bf16[8,48,32,512]{3,2,1,0:T(8,128)(2,1)} async-done(((bf16[8,48,32,512]{3,2,1,0:T(8,128)(2,1)}), bf16[8,48,32,512]{3,2,1,0:T(8,128)(2,1)}, u32[]{:S(2)}, u32[]{:S(2)}) %all-to-all-start.1) | async-done | bytes 12582944 | tf_op jit(solution)/shard_map/all_to_all | solution.py:214
  325.0 27.6 %middle.1 = (bf16[8,48,32,512]{3,2,1,0:T(8,128)(2,1)}, f32[48,256,1]{2,1,0:T(8,128)}, f32[256,256]{1,0:T(8,128)}, f32[256,256]{1,0:T(8,128)}) custom-call(bf16[8,48,32,512]{3,2,1,0:T(8,128)(2,1)} %all-to-all-done.first_ref, bf16[8,48,32,512]{3,2,1,0:T(8,128)(2,1)} %all-to-all-done.1.grad_ref, bf16[256,256]{1,0:T(8,128)(2,1)S(1)} %copy-done.7, ...), custom_call_target="tpu_custom_call" | custom-call | flops 16106127360 | bytes 37748736 | tf_op jit(solution)/shard_map/middle/pallas_call | solution.py:162
  352.7 5.4 all-to-all-start.2
  358.1 20.3 %second.1 = bf16[8,48,32,512]{3,2,1,0:T(8,128)(2,1)} custom-call(bf16[8,48,32,512]{3,2,1,0:T(8,128)(2,1)} %all-to-all-done.first_ref, bf16[256,256]{1,0:T(8,128)(2,1)S(1)} %copy-done.7, bf16[256,256]{1,0:T(8,128)(2,1)S(1)} %copy-done.8, f32[48,256,1]{2,1,0:T(8,128)} %copy.22.rows_ref), custom_call_target="tpu_custom_call" | custom-call | flops 6442450944 | bytes 25165824 | tf_op jit(solution)/shard_map/second/pallas_call | solution.py:162
  378.4 0.0 copy-start.3
  378.4 0.0 copy-start.5
  378.4 118.6 %all-to-all-done.2 = bf16[8,48,32,512]{3,2,1,0:T(8,128)(2,1)} async-done(((bf16[8,48,32,512]{3,2,1,0:T(8,128)(2,1)}), bf16[8,48,32,512]{3,2,1,0:T(8,128)(2,1)}, u32[]{:S(2)}, u32[]{:S(2)}) %all-to-all-start.2) | async-done | bytes 12582944 | tf_op jit(solution)/shard_map/all_to_all | solution.py:214
  497.1 5.4 all-to-all-start.3
  502.4 0.0 all-reduce.7.cloned.1.call-start
  502.5 0.0 copy-done.3
  502.5 0.2 copy.23
  502.7 4.5 reduce
  507.2 0.0 copy-start.9
  507.2 0.0 copy-done.5
  507.2 47.7 %input.1 = (bf16[384,16384]{1,0:T(8,128)(2,1)}, f32[384,512]{1,0:T(8,128)}, f32[512,512]{1,0:T(8,128)}) custom-call(bf16[384,32,512]{2,1,0:T(8,128)(2,1)} %bitcast.5.grad_ref, bf16[384,16384]{1,0:T(8,128)(2,1)} %in_ref.3, bf16[512,512]{1,0:T(8,128)(2,1)S(1)} %copy-done.3, bf16[512,512]{1,0:T(8,128)(2,1)S(1)} %bitcast.9, f32[384,512]{1,0:T(8,128)S(1)} %copy-done.5), custom_call_target="tpu_custom_call" | custom-call | flops 19327352832 | bytes 37748736 | tf_op jit(solution)/shard_map/input/pallas_call | solution.py:162
  555.0 0.0 copy-done.9
  555.0 0.0 all-reduce.7.cloned.1.call-update
  555.0 0.0 all-reduce.5.cloned.1.call-start
  555.0 99.0 %all-to-all-done.3 = bf16[8,48,32,512]{3,2,1,0:T(8,128)(2,1)} async-done(((bf16[8,48,32,512]{3,2,1,0:T(8,128)(2,1)}), bf16[8,48,32,512]{3,2,1,0:T(8,128)(2,1)}, u32[]{:S(2)}, u32[]{:S(2)}) %all-to-all-start.3) | async-done | bytes 12582944 | tf_op jit(solution)/shard_map/all_to_all | solution.py:214
  654.0 33.7 %gating.1 = (bf16[384,16384]{1,0:T(8,128)(2,1)}, f32[512,512]{1,0:T(8,128)}) custom-call(bf16[384,32,512]{2,1,0:T(8,128)(2,1)} %bitcast.7.second_ref, bf16[384,16384]{1,0:T(8,128)(2,1)} %up_ref.3, bf16[384,16384]{1,0:T(8,128)(2,1)} %gate_ref.3, bf16[512,512]{1,0:T(8,128)(2,1)S(1)} %copy-done.6), custom_call_target="tpu_custom_call" | custom-call | flops 12884901888 | bytes 50331648 | tf_op jit(solution)/shard_map/gating/pallas_call | solution.py:162
  687.7 0.0 all-reduce.5.cloned.1.call-update
  687.7 0.0 all-reduce.7.cloned.1.call-done
  687.8 1.8 broadcast_multiply_fusion.3
  689.5 2.1 broadcast_multiply_fusion.2
  691.6 133.4 %all-reduce.5.cloned.1.call-done = (f32[512,512]{1,0:T(8,128)}, f32[256,256]{1,0:T(8,128)}, f32[256,256]{1,0:T(8,128)}, f32[512,512]{1,0:T(8,128)}) async-done(((f32[512,512]{1,0:T(8,128)}, f32[256,256]{1,0:T(8,128)}, f32[256,256]{1,0:T(8,128)}, f32[512,512]{1,0:T(8,128)}), (f32[512,512]{1,0:T(8,128)}, f32[256,256]{1,0:T(8,128)}, f32[256,256]{1,0:T(8,128)}, ...) | async-done | bytes 2621456 | tf_op jit(solution)/shard_map/psum | solution.py:262
  825.0 1.9 broadcast_multiply_fusion.4
  826.9 3.1 broadcast_multiply_fusion
  830.0 0.0 copy-done.1
  (4 shorter events, 0.1 us)
Async XLA Ops:
  7.2 178.9 %copy-start = (f32[384,256]{1,0:T(8,128)S(1)}, f32[384,256]{1,0:T(8,128)}, u32[]{:S(2)}) copy-start(f32[384,256]{1,0:T(8,128)} %param.17) | copy-start | bytes 1179652
  7.2 1.1 copy-start.2
  8.3 1.1 copy-start.4
  35.3 5.5 copy-start.6
  35.3 145.2 %all-to-all-start = ((bf16[8,48,32,512]{3,2,1,0:T(8,128)(2,1)}), bf16[8,48,32,512]{3,2,1,0:T(8,128)(2,1)}, u32[]{:S(2)}, u32[]{:S(2)}) async-start(bf16[8,48,32,512]{3,2,1,0:T(8,128)(2,1)} %bitcast.12), calls=%async_computation | async-start | bytes 25165824 | tf_op jit(solution)/shard_map/all_to_all | solution.py:214
  180.6 9.5 %copy-start.7 = (bf16[256,256]{1,0:T(8,128)(2,1)S(1)}, bf16[256,256]{1,0:T(8,128)(2,1)}, u32[]{:S(2)}) copy-start(bf16[256,256]{1,0:T(8,128)(2,1)} %two_ref.3) | copy-start | bytes 393220
  180.6 9.6 %copy-start.8 = (bf16[256,256]{1,0:T(8,128)(2,1)S(1)}, bf16[256,256]{1,0:T(8,128)(2,1)}, u32[]{:S(2)}) copy-start(bf16[256,256]{1,0:T(8,128)(2,1)} %three_ref.1) | copy-start | bytes 393220
  180.6 144.5 %all-to-all-start.1 = ((bf16[8,48,32,512]{3,2,1,0:T(8,128)(2,1)}), bf16[8,48,32,512]{3,2,1,0:T(8,128)(2,1)}, u32[]{:S(2)}, u32[]{:S(2)}) async-start(bf16[8,48,32,512]{3,2,1,0:T(8,128)(2,1)} %bitcast.13), calls=%async_computation.1 | async-start | bytes 25165824 | tf_op jit(solution)/shard_map/all_to_all | solution.py:214
  352.7 144.4 %all-to-all-start.2 = ((bf16[8,48,32,512]{3,2,1,0:T(8,128)(2,1)}), bf16[8,48,32,512]{3,2,1,0:T(8,128)(2,1)}, u32[]{:S(2)}, u32[]{:S(2)}) async-start(bf16[8,48,32,512]{3,2,1,0:T(8,128)(2,1)} %get-tuple-element.17), calls=%async_computation.2 | async-start | bytes 25165824 | tf_op jit(solution)/shard_map/all_to_all | solution.py:214
  378.4 124.1 %copy-start.3 = (bf16[512,512]{1,0:T(8,128)(2,1)S(1)}, bf16[512,512]{1,0:T(8,128)(2,1)}, u32[]{:S(2)}) copy-start(bf16[512,512]{1,0:T(8,128)(2,1)} %one_ref.3) | copy-start | bytes 1572868
  378.4 128.8 %copy-start.5 = (f32[384,512]{1,0:T(8,128)S(1)}, f32[384,512]{1,0:T(8,128)}, u32[]{:S(2)}) copy-start(f32[384,512]{1,0:T(8,128)} %cols_ref.3) | copy-start | bytes 2359300
  497.1 157.0 %all-to-all-start.3 = ((bf16[8,48,32,512]{3,2,1,0:T(8,128)(2,1)}), bf16[8,48,32,512]{3,2,1,0:T(8,128)(2,1)}, u32[]{:S(2)}, u32[]{:S(2)}) async-start(bf16[8,48,32,512]{3,2,1,0:T(8,128)(2,1)} %second.1), calls=%async_computation.3 | async-start | bytes 25165824 | tf_op jit(solution)/shard_map/all_to_all | solution.py:214
  502.4 185.3 %all-reduce.7.cloned.1.call-start = ((), (), s32[]{:S(2)}) async-start(), calls=%async_computation.5 | async-start | bytes 2359296 | tf_op jit(solution)/shard_map/psum | solution.py:261
  507.2 47.7 %copy-start.9 = (f32[384,256]{1,0:T(8,128)}, f32[384,256]{1,0:T(8,128)S(1)}, u32[]{:S(2)}) copy-start(f32[384,256]{1,0:T(8,128)S(1)} %constant_dynamic-update-slice_fusion) | copy-start | bytes 1179652
  555.0 270.0 %all-reduce.5.cloned.1.call-start = ((), (), s32[]{:S(2)}) async-start(), calls=%async_computation.4 | async-start | bytes 5242880 | tf_op jit(solution)/shard_map/psum | solution.py:262
  654.0 175.9 %copy-start.1 = (f32[384,256]{1,0:T(8,128)S(1)}, f32[384,256]{1,0:T(8,128)}, u32[]{:S(2)}) copy-start(f32[384,256]{1,0:T(8,128)} %param.17) | copy-start | bytes 1179652
Sparse Core Ops, SparseCore 0:
  555.1 97.2 all-reduce.6
  687.8 137.1 all-reduce.4
